TPU v7x, 32 devices: a whole 2x2x4 slice. The times are simulated.
32 devices in a mesh: grp: 2 (over x), scan: 16 (over z, y, core).
Axes of the slice: x: 2, y: 2, z: 4, core: 2. Of those that a mesh axis runs over, the one named last changes fastest.
Arguments:
- patterns: bfloat16 [3072, 64, 256], P(('grp', 'scan')), parts along dimension 0, may hold values from -6 to 6
- templates: bfloat16 [32, 64, 256], P('scan'), may hold values from -6 to 6
- radius_bin: int32 [64], replicated, may hold values from 0 to 7
- radial_gain: float32 [8], replicated, may hold values from 0.25 to 4
- orientation: int32 [32, 1], replicated, may hold values from 0 to 15
Outputs:
- corr_map: float32 [3072, 32], P(('grp', 'scan')), parts along dimension 0
- orient_map: float32 [3072, 16], P(('grp', 'scan')), parts along dimension 0
There are 2 independent parts, one for each index of `grp`. A program takes and returns all parts, laid end to end along the dimension named above; an argument that names none is the same for every part. Nothing has to cross between parts.
Inputs may be any that keep to these rules, and one draw needn't show every extreme that they name: Every orientation group holds at least one template.
All inputs are finite; a program needn't handle non-finite values.
Results may differ from a plain program's by a relative error of at most 0.0024.
Values may be sent and summed in bfloat16 or wider, within the bound.
No kernel may reach another device: no remote copies, remote signals or barrier semaphores. Data moves between devices by JAX's collectives and lax.ppermute only.
A program may use at most 128 MiB of HBM per device.

v0:
```python
import math
import jax
import jax.numpy as jnp
from jax import lax
from jax.sharding import PartitionSpec as P

RADII = 64
ANGLES = 256
GAINS = 8
TMPL_PER_GROUP = 2


def with_halo(shard, sides, width):
    for axis, dim in sides:
        size, length = (lax.axis_size(axis), shard.shape[dim])
        up = [(i, (i + 1) % size) for i in range(size - 1)]
        down = [(j, i) for i, j in up]
        last = lax.slice_in_dim(shard, length - width, length, axis=dim)
        leading = lax.slice_in_dim(shard, 0, width, axis=dim)
        before = lax.ppermute(last, axis, up)
        after = lax.ppermute(leading, axis, down)
        shard = jnp.concatenate([before, shard, after], axis=dim)
    return shard


def make_tables():
    half = ANGLES // 2
    along = jnp.arange(ANGLES, dtype=jnp.int32)
    modes = jnp.arange(half + 1, dtype=jnp.int32)
    phase = 2.0 * math.pi / ANGLES * (along[:, None] * modes[None, :] % ANGLES).astype(jnp.float32)
    basis = jnp.concatenate([jnp.cos(phase), jnp.sin(phase[:, 1:half])], axis=1).astype(
        jnp.bfloat16
    )
    factor_norm = 1.0 / (ANGLES * math.sqrt(RADII * ANGLES))
    mode_weight = jnp.where((modes == 0) | (modes == half), 1.0, 2.0).astype(jnp.float32)
    phase_rows = phase.T
    inverse = jnp.concatenate(
        [mode_weight[:, None] * jnp.cos(phase_rows), -mode_weight[:, None] * jnp.sin(phase_rows)],
        axis=0,
    )
    return (basis, (inverse * factor_norm).astype(jnp.bfloat16))


def spectrum(raw, basis):
    count = raw.shape[0]
    flat = raw.reshape(-1, ANGLES)
    spec = lax.dot_general(
        basis, flat, (((0,), (1,)), ((), ())), preferred_element_type=jnp.float32
    )
    return spec.reshape(ANGLES, count, RADII)


def mode_products(left, right):
    return jnp.einsum("kpr,ktr->ktp", left, right, preferred_element_type=jnp.float32)


def correlate(pat_spec, tmpl_spec, inverse):
    half = ANGLES // 2
    count = tmpl_spec.shape[1]
    pos_count = pat_spec.shape[1]
    pat_cos = pat_spec[: half + 1]
    pat_sin = pat_spec[half + 1 :]
    tmpl_cos = tmpl_spec[: half + 1]
    tmpl_sin = tmpl_spec[half + 1 :]
    both_cos = mode_products(pat_cos, tmpl_cos)
    both_sin = mode_products(pat_sin, tmpl_sin)
    cos_sin = mode_products(pat_cos[1:half], tmpl_sin)
    sin_cos = mode_products(pat_sin, tmpl_cos[1:half])
    edge = jnp.zeros((1, count, pos_count), jnp.float32)
    real_part = both_cos + jnp.concatenate([edge, both_sin, edge], axis=0)
    imag_part = jnp.concatenate([edge, cos_sin - sin_cos, edge], axis=0)
    cross = jnp.concatenate([real_part, imag_part], axis=0).astype(jnp.bfloat16)
    cross = cross.reshape(2 * (half + 1), count * pos_count)
    shifted = lax.dot_general(
        inverse, cross, (((0,), (0,)), ((), ())), preferred_element_type=jnp.float32
    )
    return jnp.max(shifted, axis=0).reshape(count, pos_count)


def block_of(count, limit):
    size = limit
    while size > 1:
        if count % size == 0:
            return size
        size = size // 2
    return 1


def correlate_into(carry, pat_spec, count, prepare, inverse):
    block_size = block_of(count, 64)

    def step(index, total):
        begin = index * block_size
        values = correlate(pat_spec, prepare(begin, block_size), inverse)
        return lax.dynamic_update_slice(total, values, (begin, jnp.int32(0)))

    return lax.fori_loop(0, count // block_size, step, carry)


def on_device(patterns, templates, radius_bin, radial_gain, orientation):
    basis, inverse = make_tables()
    pos_count = patterns.shape[0]
    total_tmpl = templates.shape[0] * lax.axis_size("scan")
    group_count = total_tmpl // TMPL_PER_GROUP
    onehot = (radius_bin[:, None] == jnp.arange(GAINS, dtype=jnp.int32)[None, :]).astype(
        jnp.float32
    )
    radius_weight = jnp.sum(onehot * radial_gain[None, :], axis=1)
    pat_spec = (spectrum(patterns, basis) * radius_weight[None, None, :]).astype(jnp.bfloat16)
    initial = jnp.zeros((total_tmpl, pos_count), jnp.float32)

    def raw_rows(piece):
        return lambda begin, size: spectrum(
            lax.dynamic_slice_in_dim(piece, begin, size, 0), basis
        ).astype(jnp.bfloat16)

    piece = lax.all_gather(templates, "scan", axis=0, tiled=True)
    by_template = correlate_into(initial, pat_spec, piece.shape[0], raw_rows(piece), inverse)
    corr_map = by_template.T
    groups = orientation[:, 0]
    member = groups[None, :] == jnp.arange(group_count, dtype=jnp.int32)[:, None]
    group_block = block_of(group_count, 16)
    member_blocks = member.reshape(group_count // group_block, group_block, total_tmpl)

    def group_max(mask):
        return jnp.max(jnp.where(mask[:, :, None], by_template[None, :, :], -jnp.inf), axis=1)

    best = lax.map(group_max, member_blocks).reshape(group_count, pos_count).T
    padded = with_halo(best, (("scan", 0),), 1)
    orient_map = 0.25 * (padded[:-2] + 2.0 * best + padded[2:])
    return (corr_map, orient_map)


def solution(mesh):
    placed = (P(("grp", "scan"), None, None), P("scan", None, None), P(), P(), P())
    return jax.shard_map(
        on_device,
        mesh=mesh,
        in_specs=placed,
        out_specs=(P(("grp", "scan"), None), P(("grp", "scan"), None)),
        check_vma=False,
    )
```

profile of v0, /device:TPU:5, one launch (start us, length us, event | category | flops | bytes accessed | tf_op | source)
XLA Modules:
  0.0 101.3 jit_solution(18244889343172042133)
XLA Ops:
  7.2 0.7 all-gather.2.cloned.1.call-update
  7.9 1.0 select_reduce_fusion.1
  8.9 1.0 cosine_convert_fusion
  9.8 0.1 fusion.19
  10.0 0.5 fusion.31
  10.5 3.6 %multiply_convert_fusion = bf16[256,96,64]{0,1,2:T(8,128)(2,1)S(1)} fusion(f32[64]{0:T(128)S(1)} %select_reduce_fusion.1, bf16[96,64,256]{2,1,0:T(8,128)(2,1)S(1)} %copy-done, bf16[256,127]{1,0:T(8,128)(2,1)S(1)} %fusion.31, bf16[256,129]{1,0:T(8,128)(2,1)S(1)} %cosine_convert_fusion), kind=kOutput, calls=%fused_computation | convolution fusion | flops 808714240 | bytes 6422784 | tf_op jit(solution)/shard_map/dot_general | solution.py:47
  14.1 2.7 %fusion.41 = (bf16[127,96,64]{0,1,2:T(8,128)(2,1)}, bf16[127,96,64]{0,1,2:T(8,128)(2,1)}) fusion(bf16[256,96,64]{0,1,2:T(8,128)(2,1)S(1)} %multiply_convert_fusion), kind=kLoop, calls=%fused_computation.59 | loop fusion | bytes 6242304 | tf_op jit(solution)/shard_map/while/body/eval_jaxpr/slice | solution.py:62
  16.9 4.0 %copy.44 = bf16[127,96,64]{1,2,0:T(8,128)(2,1)} copy(bf16[127,96,64]{0,1,2:T(8,128)(2,1)} %get-tuple-element.28) | data formatting | bytes 3121152 | tf_op jit(solution)/shard_map/while/body/eval_jaxpr/slice | solution.py:67
  20.9 4.0 %copy.42 = bf16[127,96,64]{1,2,0:T(8,128)(2,1)} copy(bf16[127,96,64]{0,1,2:T(8,128)(2,1)} %get-tuple-element.20) | data formatting | bytes 3121152 | tf_op jit(solution)/shard_map/while/body/eval_jaxpr/slice | solution.py:62
  24.9 5.0 %copy.40 = bf16[129,96,64]{1,2,0:T(8,128)(2,1)} copy(bf16[129,96,64]{0,1,2:T(8,128)(2,1)} %bitcast.19) | data formatting | bytes 3170304 | tf_op jit(solution)/shard_map/while/body/eval_jaxpr/slice | solution.py:61
  29.9 1.2 %sine_multiply_fusion = (f32[129,256]{1,0:T(8,128)S(1)}, f32[129,256]{1,0:T(8,128)}) fusion(f32[129]{0:T(256)S(1)} %fusion.35, f32[129]{0:T(256)S(1)} %or_select_fusion), kind=kLoop, calls=%fused_computation.35 | loop fusion | flops 528384 | bytes 265224 | tf_op jit(solution)/shard_map/mul | solution.py:38
  31.1 17.7 %all-gather.2.cloned.1.call-done = bf16[32,64,256]{2,1,0:T(8,128)(2,1)} async-done(((bf16[2,64,256]{2,1,0:T(8,128)(2,1)}), bf16[32,64,256]{2,1,0:T(8,128)(2,1)}) %all-gather.2.cloned.1.call-update) | async-done | bytes 1048592 | tf_op jit(solution)/shard_map/all_gather | solution.py:117
  48.8 1.7 %convolution_convert_fusion = bf16[256,32,64]{0,2,1:T(8,128)(2,1)S(1)} fusion(bf16[32,64,256]{2,1,0:T(8,128)(2,1)} %all-gather.2.cloned.1.call-done, bf16[256,127]{1,0:T(8,128)(2,1)S(1)} %fusion.31, bf16[256,129]{1,0:T(8,128)(2,1)S(1)} %cosine_convert_fusion), kind=kOutput, calls=%fused_computation.14 | convolution fusion | flops 269221888 | bytes 2228224 | tf_op jit(solution)/shard_map/while/body/eval_jaxpr/dot_general | solution.py:47
  50.6 0.9 copy-done.3
  51.5 1.4 %fusion.42 = (bf16[127,32,64]{0,2,1:T(8,128)(2,1)}, bf16[127,32,64]{0,2,1:T(8,128)(2,1)}) fusion(bf16[256,32,64]{0,2,1:T(8,128)(2,1)S(1)} %convolution_convert_fusion), kind=kLoop, calls=%fused_computation.60 | loop fusion | bytes 2080768 | tf_op jit(solution)/shard_map/while/body/eval_jaxpr/slice | solution.py:68
  52.9 3.5 %copy.41 = bf16[127,32,64]{2,1,0:T(8,128)(2,1)} copy(bf16[127,32,64]{0,2,1:T(8,128)(2,1)} %get-tuple-element.30) | data formatting | bytes 1040384 | tf_op jit(solution)/shard_map/while/body/eval_jaxpr/slice | solution.py:64
  56.4 3.5 %copy.45 = bf16[127,32,64]{2,1,0:T(8,128)(2,1)} copy(bf16[127,32,64]{0,2,1:T(8,128)(2,1)} %get-tuple-element.29) | data formatting | bytes 1040384 | tf_op jit(solution)/shard_map/while/body/eval_jaxpr/slice | solution.py:68
  59.9 2.7 %fusion.45 = f32[127,32,96]{2,1,0:T(8,128)S(1)} fusion(bf16[127,32,64]{2,1,0:T(8,128)(2,1)} %copy.41, bf16[127,96,64]{1,2,0:T(8,128)(2,1)} %copy.44), kind=kOutput, calls=%fused_computation.63 | convolution fusion | flops 49938432 | bytes 3641344 | tf_op jit(solution)/shard_map/while/body/eval_jaxpr/kpr,ktr->ktp/dot_general | solution.py:54
  62.7 2.0 %fusion.44 = f32[127,32,96]{2,1,0:T(8,128)} fusion(bf16[127,32,64]{2,1,0:T(8,128)(2,1)S(1)} %copy-done.4, bf16[127,96,64]{1,2,0:T(8,128)(2,1)S(1)} %copy-done.1), kind=kOutput, calls=%fused_computation.62 | convolution fusion | flops 49938432 | bytes 3641344 | tf_op jit(solution)/shard_map/while/body/eval_jaxpr/kpr,ktr->ktp/dot_general | solution.py:54
  64.7 1.7 %subtract_convert_fusion = bf16[127,32,96]{2,1,0:T(8,128)(2,1)} fusion(f32[127,32,96]{2,1,0:T(8,128)S(1)} %fusion.45, bf16[127,32,64]{2,1,0:T(8,128)(2,1)S(1)} %copy-done.5, bf16[127,96,64]{1,2,0:T(8,128)(2,1)S(1)} %copy-done.1), kind=kOutput, calls=%fused_computation.5 | convolution fusion | flops 50718720 | bytes 4421632 | tf_op jit(solution)/shard_map/while/body/eval_jaxpr/kpr,ktr->ktp/dot_general | solution.py:54
  66.4 2.7 %copy.47 = bf16[127,32,96]{0,2,1:T(8,128)(2,1)} copy(bf16[127,32,96]{2,1,0:T(8,128)(2,1)} %subtract_convert_fusion) | data formatting | bytes 1560576 | tf_op jit(solution)/shard_map/convert.4
  69.1 2.4 %copy.48 = bf16[127,3072]{1,0:T(8,128)(2,1)} copy(bf16[127,3072]{0,1:T(8,128)(2,1)} %bitcast.21) | data formatting | bytes 1560576 | tf_op jit(solution)/shard_map/while/body/eval_jaxpr/concatenate | solution.py:72
  71.5 2.8 %copy.39 = bf16[129,32,64]{2,1,0:T(8,128)(2,1)} copy(bf16[129,32,64]{0,2,1:T(8,128)(2,1)} %bitcast.20) | data formatting | bytes 1056768 | tf_op jit(solution)/shard_map/while/body/eval_jaxpr/slice | solution.py:63
  74.3 4.3 %fusion.4 = bf16[129,32,96]{2,1,0:T(8,128)(2,1)} fusion(f32[1,32,96]{2,1,0:T(8,128)S(1)} %broadcast.63, f32[127,32,96]{2,1,0:T(8,128)} %fusion.44, bf16[129,32,64]{2,1,0:T(8,128)(2,1)} %copy.39, bf16[129,96,64]{1,2,0:T(8,128)(2,1)} %copy.40), kind=kOutput, calls=%fused_computation.4 | convolution fusion | flops 52310016 | bytes 4478976 | tf_op jit(solution)/shard_map/while/body/eval_jaxpr/kpr,ktr->ktp/dot_general | solution.py:54
  78.6 3.4 %concatenate.33 = bf16[129,3072]{1,0:T(8,128)(2,1)} reshape(bf16[129,32,96]{2,1,0:T(8,128)(2,1)} %fusion.4) | data formatting | bytes 1585152 | tf_op jit(solution)/shard_map/while/body/eval_jaxpr/concatenate | solution.py:72
  82.0 2.5 %fusion.13 = f32[3072]{0:T(1024)S(1)} fusion(bf16[1,3072]{1,0:T(2,128)(2,1)S(1)} %concatenate.34, bf16[127,3072]{1,0:T(8,128)(2,1)} %copy.48, bf16[129,3072]{1,0:T(8,128)(2,1)} %concatenate.33, f32[129,256]{1,0:T(8,128)S(1)} %get-tuple-element.37, f32[129,256]{1,0:T(8,128)S(1)} %copy-done.6), kind=kOutput, calls=%fused_computation.15 | convolution fusion | flops 413121024 | bytes 1855488 | tf_op jit(solution)/shard_map/while/body/eval_jaxpr/dot_general | solution.py:74
  84.5 0.1 select_reduce_fusion
  84.6 0.1 fusion.43
  84.7 3.2 %collective-permute-start = (f32[1,16]{0,1:T(8,128)S(1)}, f32[1,16]{0,1:T(8,128)S(1)}, u32[]{:S(2)}, u32[]{:S(2)}) collective-permute-start(f32[1,16]{0,1:T(8,128)S(1)} %get-tuple-element.31), channel_id=1, source_target_pairs={{0,1},{1,2},{2,3},{3,4},{4,5},{5,6},{6,7},{7,8},{8,9},{9,10},{10,1... | collective-permute-start | bytes 200 | tf_op jit(solution)/shard_map/ppermute | solution.py:20
  87.9 1.9 %collective-permute-start.1 = (f32[1,16]{0,1:T(8,128)S(1)}, f32[1,16]{0,1:T(8,128)S(1)}, u32[]{:S(2)}, u32[]{:S(2)}) collective-permute-start(f32[1,16]{0,1:T(8,128)S(1)} %get-tuple-element.36), channel_id=1, source_target_pairs={{1,0},{2,1},{3,2},{4,3},{5,4},{6,5},{7,6},{8,7},{9,8},{10,9},{11,1... | collective-permute-start | bytes 200 | tf_op jit(solution)/shard_map/ppermute | solution.py:21
  89.9 3.9 %collective-permute-done.1 = f32[1,16]{0,1:T(8,128)S(1)} collective-permute-done((f32[1,16]{0,1:T(8,128)S(1)}, f32[1,16]{0,1:T(8,128)S(1)}, u32[]{:S(2)}, u32[]{:S(2)}) %collective-permute-start.1) | collective-permute-done | bytes 96 | tf_op jit(solution)/shard_map/ppermute | solution.py:21
  93.8 0.7 fusion.33
  (25 shorter events, 0.2 us)
Async XLA Ops:
  7.2 3.3 %copy-start = (bf16[96,64,256]{2,1,0:T(8,128)(2,1)S(1)}, bf16[96,64,256]{2,1,0:T(8,128)(2,1)}, u32[]{:S(2)}) copy-start(bf16[96,64,256]{2,1,0:T(8,128)(2,1)} %param.5) | copy-start | bytes 9437188
  7.2 41.6 %all-gather.2.cloned.1.call-start = ((), (), s32[]{:S(2)}) async-start(), calls=%async_computation | async-start | bytes 1114112 | tf_op jit(solution)/shard_map/all_gather | solution.py:117
  14.1 2.7 %copy-start.2 = (bf16[256,96,64]{0,1,2:T(8,128)(2,1)}, bf16[256,96,64]{0,1,2:T(8,128)(2,1)S(1)}, u32[]{:S(2)}) copy-start(bf16[256,96,64]{0,1,2:T(8,128)(2,1)S(1)} %multiply_convert_fusion) | copy-start | bytes 9437188
  24.9 5.0 %copy-start.8 = (s32[32,1]{0,1:T(1,128)S(1)}, s32[32,1]{0,1:T(1,128)}, u32[]{:S(2)}) copy-start(s32[32,1]{0,1:T(1,128)} %param.9) | copy-start | bytes 388
  50.6 1.0 copy-start.3
  59.9 2.7 %copy-start.1 = (bf16[127,96,64]{1,2,0:T(8,128)(2,1)S(1)}, bf16[127,96,64]{1,2,0:T(8,128)(2,1)}, u32[]{:S(2)}) copy-start(bf16[127,96,64]{1,2,0:T(8,128)(2,1)} %copy.42) | copy-start | bytes 4681732
  59.9 2.8 %copy-start.4 = (bf16[127,32,64]{2,1,0:T(8,128)(2,1)S(1)}, bf16[127,32,64]{2,1,0:T(8,128)(2,1)}, u32[]{:S(2)}) copy-start(bf16[127,32,64]{2,1,0:T(8,128)(2,1)} %copy.41) | copy-start | bytes 1560580
  62.7 2.0 %copy-start.5 = (bf16[127,32,64]{2,1,0:T(8,128)(2,1)S(1)}, bf16[127,32,64]{2,1,0:T(8,128)(2,1)}, u32[]{:S(2)}) copy-start(bf16[127,32,64]{2,1,0:T(8,128)(2,1)} %copy.45) | copy-start | bytes 1560580
  74.3 7.6 %copy-start.6 = (f32[129,256]{1,0:T(8,128)S(1)}, f32[129,256]{1,0:T(8,128)}, u32[]{:S(2)}) copy-start(f32[129,256]{1,0:T(8,128)} %get-tuple-element.38) | copy-start | bytes 396292
  84.5 10.0 %copy-start.7 = (f32[32,96]{1,0:T(8,128)}, f32[32,96]{1,0:T(8,128)S(1)}, u32[]{:S(2)}) copy-start(f32[32,96]{1,0:T(8,128)S(1)} %reshape.51) | copy-start | bytes 36868
  84.7 5.2 %collective-permute-start = (f32[1,16]{0,1:T(8,128)S(1)}, f32[1,16]{0,1:T(8,128)S(1)}, u32[]{:S(2)}, u32[]{:S(2)}) collective-permute-start(f32[1,16]{0,1:T(8,128)S(1)} %get-tuple-element.31), channel_id=1, source_target_pairs={{0,1},{1,2},{2,3},{3,4},{4,5},{5,6},{6,7},{7,8},{8,9},{9,10},{10,1... | collective-permute-start | bytes 200 | tf_op jit(solution)/shard_map/ppermute | solution.py:20
  87.9 5.9 %collective-permute-start.1 = (f32[1,16]{0,1:T(8,128)S(1)}, f32[1,16]{0,1:T(8,128)S(1)}, u32[]{:S(2)}, u32[]{:S(2)}) collective-permute-start(f32[1,16]{0,1:T(8,128)S(1)} %get-tuple-element.36), channel_id=1, source_target_pairs={{1,0},{2,1},{3,2},{4,3},{5,4},{6,5},{7,6},{8,7},{9,8},{10,9},{11,1... | collective-permute-start | bytes 200 | tf_op jit(solution)/shard_map/ppermute | solution.py:21
Sparse Core Ops, SparseCore 0:
  10.2 38.5 all-gather.1
where the time goes:
time: 102 us; the launch traced here: 101 us
  local copies, waits for them, and re-layouts  36.6 us (36%)
  waiting for transfers between devices  22.3 us (22%)
  matrix products  18.5 us (18%)
  between operations  14.2 us (14%)
  starting transfers between devices  5.19 us (5%)
  other arithmetic  4.61 us (5%)
    all_gather x1, waiting for transfers between devices, on_device(): piece = lax.all_gather(templates, 'scan', axis=0, tiled=True)  17.7 us
    dot_general x4, matrix products, mode_products(): jnp.einsum('kpr,ktr->ktp', left, right, preferred_element_type=jnp.float32)  10.6 us
    slice x2, local copies, waits for them, and re-layouts, correlate(): pat_sin = pat_spec[half + 1:]  6.72 us
    concatenate x3, local copies, waits for them, and re-layouts, correlate(): cross = jnp.concatenate([real_part, imag_part], axis=0).astype(jnp.bfloat16)  5.75 us
    dot_general x2, matrix products, spectrum(): lax.dot_general(basis, flat, (((0,), (1,)), ((), ())), preferred_element_...  5.37 us
    slice x1, local copies, waits for them, and re-layouts, correlate(): pat_cos = pat_spec[:half + 1]  4.96 us
    slice x2, local copies, waits for them, and re-layouts, correlate(): sin_cos = mode_products(pat_sin, tmpl_cos[1:half])  4.9 us
    slice x1, local copies, waits for them, and re-layouts, correlate(): cos_sin = mode_products(pat_cos[1:half], tmpl_sin)  4 us
  transfers between devices with their start and end apart: 3, of which 2 were waited for; matrix products, arithmetic and copies ran while one was open for 23% of the time, Pallas kernels for 0%

commit v1 on v0

--- a/solution.py
+++ b/solution.py
@@ -8,6 +8,31 @@
 ANGLES = 256
 GAINS = 8
 TMPL_PER_GROUP = 2
+
+
+def squares_render(patch, join_dim):
+    patch = jnp.moveaxis(patch, 0, join_dim)
+    t1 = patch.shape
+    latest = patch.reshape(*t1[:join_dim], t1[join_dim] * t1[join_dim + 1], *t1[join_dim + 2 :])
+    return latest
+
+
+def see_stages_all(matrix, named_axis):
+    val2 = lax.axis_size(named_axis)
+    parts_out = lax.axis_index(named_axis)
+    found_now, block_last = (val2, parts_out)
+    state_next, now = (matrix[None], 1)
+    while now < found_now:
+        sheets = []
+        for to_i in [*range(found_now)]:
+            sheets.append((to_i, to_i ^ now))
+        n_now = lax.ppermute(state_next, axis_name=named_axis, perm=sheets)
+        upper = block_last & now == 0
+        x_new = jnp.where(upper, state_next, n_now)
+        odd = jnp.where(upper, n_now, state_next)
+        state_next = jnp.concatenate([x_new, odd])
+        now *= 2
+    return state_next
 
 
 def with_halo(shard, sides, width):
@@ -114,7 +139,7 @@
             lax.dynamic_slice_in_dim(piece, begin, size, 0), basis
         ).astype(jnp.bfloat16)
 
-    piece = lax.all_gather(templates, "scan", axis=0, tiled=True)
+    piece = squares_render(see_stages_all(templates, "scan"), 0)
     by_template = correlate_into(initial, pat_spec, piece.shape[0], raw_rows(piece), inverse)
     corr_map = by_template.T
     groups = orientation[:, 0]

time: 102 us -> 105 us (1.029)
  the two profiles are of different devices: /device:TPU:5 before, /device:TPU:10 now
where the time goes in v1:
time: 105 us; the launch traced here: 104 us
  local copies, waits for them, and re-layouts  38.4 us (37%)
  waiting for transfers between devices  25.8 us (25%)
  matrix products  19.8 us (19%)
  starting transfers between devices  10.4 us (10%)
  other arithmetic  8.82 us (8%)
    ppermute x4, waiting for transfers between devices, see_stages_all(): n_now = lax.ppermute(state_next, axis_name=named_axis, perm=sheets)  21.9 us
    dot_general x4, matrix products, mode_products(): jnp.einsum('kpr,ktr->ktp', left, right, preferred_element_type=jnp.float32)  10.6 us
    slice x2, local copies, waits for them, and re-layouts, correlate(): pat_sin = pat_spec[half + 1:]  8.51 us
    dot_general x2, matrix products, spectrum(): lax.dot_general(basis, flat, (((0,), (1,)), ((), ())), preferred_element_...  6.72 us
    concatenate x3, local copies, waits for them, and re-layouts, correlate(): cross = jnp.concatenate([real_part, imag_part], axis=0).astype(jnp.bfloat16)  5.75 us
    slice x1, local copies, waits for them, and re-layouts, correlate(): pat_cos = pat_spec[:half + 1]  4.96 us
    slice x2, local copies, waits for them, and re-layouts, correlate(): sin_cos = mode_products(pat_sin, tmpl_cos[1:half])  4.88 us
    ppermute x4, starting transfers between devices, see_stages_all(): n_now = lax.ppermute(state_next, axis_name=named_axis, perm=sheets)  4.76 us
  transfers between devices with their start and end apart: 6, of which 2 were waited for; matrix products, arithmetic and copies ran while one was open for 27% of the time, Pallas kernels for 0%

profile of v1, /device:TPU:10, one launch (start us, length us, event | category | flops | bytes accessed | tf_op | source)
XLA Modules:
  0.0 104.0 jit_solution(4095707619755338960)
XLA Ops:
  0.9 1.6 %cosine_convert_fusion = bf16[256,129]{1,0:T(8,128)(2,1)} fusion(), kind=kLoop, calls=%fused_computation.30 | loop fusion | flops 495360 | bytes 66048 | tf_op jit(solution)/shard_map/convert.6
  2.5 1.1 %fusion.31 = bf16[256,127]{1,0:T(8,128)(2,1)} fusion(f32[256,129]{1,0:T(8,128)S(1)} %fusion.19), kind=kLoop, calls=%fused_computation.49 | loop fusion | flops 32512 | bytes 195072 | tf_op jit(solution)/shard_map/convert.7
  3.6 0.8 select_reduce_fusion.1
  4.4 0.9 broadcast_select_fusion.7
  5.3 1.6 %collective-permute-start.1 = (bf16[2,2,64,256]{3,2,1,0:T(8,128)(2,1)S(1)}, bf16[2,2,64,256]{3,2,1,0:T(8,128)(2,1)}, u32[]{:S(2)}, u32[]{:S(2)}) collective-permute-start(bf16[2,2,64,256]{3,2,1,0:T(8,128)(2,1)S(1)} %pad_maximum_fusion.3), channel_id=1, source_target_pairs={{0,2},{1,3},{2,0},{3,1},{4,6},{5,7},{6,4},{7,5},{8,10},{9,11},{10,... | collective-permute-start | bytes 393224 | tf_op jit(solution)/shard_map/ppermute | solution.py:29
  6.9 6.2 %multiply_convert_fusion = bf16[256,96,64]{0,1,2:T(8,128)(2,1)} fusion(f32[64]{0:T(128)S(1)} %select_reduce_fusion.1, bf16[96,64,256]{2,1,0:T(8,128)(2,1)S(1)} %copy-done, bf16[256,127]{1,0:T(8,128)(2,1)} %fusion.31, bf16[256,129]{1,0:T(8,128)(2,1)} %cosine_convert_fusion), kind=kOutput, calls=%fused_computation | convolution fusion | flops 808714240 | bytes 6422784 | tf_op jit(solution)/shard_map/dot_general | solution.py:72
  13.1 0.9 broadcast_select_fusion.5
  14.0 0.7 pad_maximum_fusion.2
  15.2 4.5 %fusion.41 = (bf16[127,96,64]{0,1,2:T(8,128)(2,1)}, bf16[127,96,64]{0,1,2:T(8,128)(2,1)}) fusion(bf16[256,96,64]{0,1,2:T(8,128)(2,1)} %multiply_convert_fusion), kind=kLoop, calls=%fused_computation.71 | loop fusion | bytes 6242304 | tf_op jit(solution)/shard_map/while/body/eval_jaxpr/slice | solution.py:87
  19.7 4.0 %copy.33 = bf16[127,96,64]{1,2,0:T(8,128)(2,1)} copy(bf16[127,96,64]{0,1,2:T(8,128)(2,1)} %get-tuple-element.28) | data formatting | bytes 3121152 | tf_op jit(solution)/shard_map/while/body/eval_jaxpr/slice | solution.py:92
  23.7 4.0 %copy.31 = bf16[127,96,64]{1,2,0:T(8,128)(2,1)} copy(bf16[127,96,64]{0,1,2:T(8,128)(2,1)} %get-tuple-element.20) | data formatting | bytes 3121152 | tf_op jit(solution)/shard_map/while/body/eval_jaxpr/slice | solution.py:87
  27.7 5.0 %copy.29 = bf16[129,96,64]{1,2,0:T(8,128)(2,1)} copy(bf16[129,96,64]{0,1,2:T(8,128)(2,1)} %bitcast.23) | data formatting | bytes 3170304 | tf_op jit(solution)/shard_map/while/body/eval_jaxpr/slice | solution.py:86
  32.7 1.0 broadcast_select_fusion.3
  33.7 2.7 %collective-permute-start.3 = (bf16[8,2,64,256]{3,2,1,0:T(8,128)(2,1)S(1)}, bf16[8,2,64,256]{3,2,1,0:T(8,128)(2,1)S(1)}, u32[]{:S(2)}, u32[]{:S(2)}) collective-permute-start(bf16[8,2,64,256]{3,2,1,0:T(8,128)(2,1)S(1)} %pad_maximum_fusion.1), channel_id=1, source_target_pairs={{0,8},{1,9},{2,10},{3,11},{4,12},{5,13},{6,14},{7,15},{8,0},{9,1},... | collective-permute-start | bytes 1572872 | tf_op jit(solution)/shard_map/ppermute | solution.py:29
  37.0 21.9 %collective-permute-done.3 = bf16[8,2,64,256]{3,2,1,0:T(8,128)(2,1)S(1)} collective-permute-done((bf16[8,2,64,256]{3,2,1,0:T(8,128)(2,1)S(1)}, bf16[8,2,64,256]{3,2,1,0:T(8,128)(2,1)S(1)}, u32[]{:S(2)}, u32[]{:S(2)}) %collective-permute-start.3) | collective-permute-done | bytes 524320 | tf_op jit(solution)/shard_map/ppermute | solution.py:29
  59.6 0.9 copy-done.2
  60.6 1.4 %fusion.42 = (bf16[127,32,64]{0,2,1:T(8,128)(2,1)}, bf16[127,32,64]{0,2,1:T(8,128)(2,1)}) fusion(bf16[256,32,64]{0,2,1:T(8,128)(2,1)S(1)} %convolution_convert_fusion), kind=kLoop, calls=%fused_computation.72 | loop fusion | bytes 2080768 | tf_op jit(solution)/shard_map/while/body/eval_jaxpr/slice | solution.py:93
  62.0 3.5 %copy.30 = bf16[127,32,64]{2,1,0:T(8,128)(2,1)} copy(bf16[127,32,64]{0,2,1:T(8,128)(2,1)} %get-tuple-element.30) | data formatting | bytes 1040384 | tf_op jit(solution)/shard_map/while/body/eval_jaxpr/slice | solution.py:89
  65.5 3.5 %copy.34 = bf16[127,32,64]{2,1,0:T(8,128)(2,1)} copy(bf16[127,32,64]{0,2,1:T(8,128)(2,1)} %get-tuple-element.29) | data formatting | bytes 1040384 | tf_op jit(solution)/shard_map/while/body/eval_jaxpr/slice | solution.py:93
  69.0 2.7 %fusion.45 = f32[127,32,96]{2,1,0:T(8,128)S(1)} fusion(bf16[127,32,64]{2,1,0:T(8,128)(2,1)} %copy.30, bf16[127,96,64]{1,2,0:T(8,128)(2,1)} %copy.33), kind=kOutput, calls=%fused_computation.75 | convolution fusion | flops 49938432 | bytes 3641344 | tf_op jit(solution)/shard_map/while/body/eval_jaxpr/kpr,ktr->ktp/dot_general | solution.py:79
  71.7 2.0 %fusion.44 = f32[127,32,96]{2,1,0:T(8,128)} fusion(bf16[127,32,64]{2,1,0:T(8,128)(2,1)S(1)} %copy-done.3, bf16[127,96,64]{1,2,0:T(8,128)(2,1)S(1)} %copy-done.1), kind=kOutput, calls=%fused_computation.74 | convolution fusion | flops 49938432 | bytes 3641344 | tf_op jit(solution)/shard_map/while/body/eval_jaxpr/kpr,ktr->ktp/dot_general | solution.py:79
  73.8 1.6 %subtract_convert_fusion = bf16[127,32,96]{2,1,0:T(8,128)(2,1)} fusion(f32[127,32,96]{2,1,0:T(8,128)S(1)} %fusion.45, bf16[127,32,64]{2,1,0:T(8,128)(2,1)S(1)} %copy-done.4, bf16[127,96,64]{1,2,0:T(8,128)(2,1)S(1)} %copy-done.1), kind=kOutput, calls=%fused_computation.5 | convolution fusion | flops 50718720 | bytes 4421632 | tf_op jit(solution)/shard_map/while/body/eval_jaxpr/kpr,ktr->ktp/dot_general | solution.py:79
  75.4 2.7 %copy.36 = bf16[127,32,96]{0,2,1:T(8,128)(2,1)} copy(bf16[127,32,96]{2,1,0:T(8,128)(2,1)} %subtract_convert_fusion) | data formatting | bytes 1560576 | tf_op jit(solution)/shard_map/convert.4
  78.1 2.4 %copy.37 = bf16[127,3072]{1,0:T(8,128)(2,1)} copy(bf16[127,3072]{0,1:T(8,128)(2,1)} %bitcast.26) | data formatting | bytes 1560576 | tf_op jit(solution)/shard_map/while/body/eval_jaxpr/concatenate | solution.py:97
  80.5 2.9 %copy.28 = bf16[129,32,64]{2,1,0:T(8,128)(2,1)} copy(bf16[129,32,64]{0,2,1:T(8,128)(2,1)} %bitcast.24) | data formatting | bytes 1056768 | tf_op jit(solution)/shard_map/while/body/eval_jaxpr/slice | solution.py:88
  83.3 4.2 %fusion.4 = bf16[129,32,96]{2,1,0:T(8,128)(2,1)} fusion(f32[1,32,96]{2,1,0:T(8,128)S(1)} %broadcast.63, f32[127,32,96]{2,1,0:T(8,128)} %fusion.44, bf16[129,32,64]{2,1,0:T(8,128)(2,1)} %copy.28, bf16[129,96,64]{1,2,0:T(8,128)(2,1)} %copy.29), kind=kOutput, calls=%fused_computation.4 | convolution fusion | flops 52310016 | bytes 4478976 | tf_op jit(solution)/shard_map/while/body/eval_jaxpr/kpr,ktr->ktp/dot_general | solution.py:79
  87.6 3.4 %concatenate.49 = bf16[129,3072]{1,0:T(8,128)(2,1)} reshape(bf16[129,32,96]{2,1,0:T(8,128)(2,1)} %fusion.4) | data formatting | bytes 1585152 | tf_op jit(solution)/shard_map/while/body/eval_jaxpr/concatenate | solution.py:97
  91.0 2.5 %fusion.13 = f32[3072]{0:T(1024)S(1)} fusion(bf16[1,3072]{1,0:T(2,128)(2,1)S(1)} %concatenate.50, bf16[127,3072]{1,0:T(8,128)(2,1)} %copy.37, bf16[129,3072]{1,0:T(8,128)(2,1)} %concatenate.49, f32[129,256]{1,0:T(8,128)S(1)} %get-tuple-element.49, f32[129,256]{1,0:T(8,128)S(1)} %get-tuple-element.50), kind=kOutput, calls=%fused_computation.15 | convolution fusion | flops 413121024 | bytes 1855488 | tf_op jit(solution)/shard_map/while/body/eval_jaxpr/dot_general | solution.py:99
  93.7 3.7 %collective-permute-start.5 = (f32[1,16]{0,1:T(8,128)S(1)}, f32[1,16]{0,1:T(8,128)S(1)}, u32[]{:S(2)}, u32[]{:S(2)}) collective-permute-start(f32[1,16]{0,1:T(8,128)S(1)} %get-tuple-element.48), channel_id=1, source_target_pairs={{1,0},{2,1},{3,2},{4,3},{5,4},{6,5},{7,6},{8,7},{9,8},{10,9},{11,1... | collective-permute-start | bytes 200 | tf_op jit(solution)/shard_map/ppermute | solution.py:46
  97.5 1.9 %collective-permute-start.4 = (f32[1,16]{0,1:T(8,128)S(1)}, f32[1,16]{0,1:T(8,128)S(1)}, u32[]{:S(2)}, u32[]{:S(2)}) collective-permute-start(f32[1,16]{0,1:T(8,128)S(1)} %get-tuple-element.47), channel_id=1, source_target_pairs={{0,1},{1,2},{2,3},{3,4},{4,5},{5,6},{6,7},{7,8},{8,9},{9,10},{10,1... | collective-permute-start | bytes 200 | tf_op jit(solution)/shard_map/ppermute | solution.py:45
  99.4 3.9 %collective-permute-done.4 = f32[1,16]{0,1:T(8,128)S(1)} collective-permute-done((f32[1,16]{0,1:T(8,128)S(1)}, f32[1,16]{0,1:T(8,128)S(1)}, u32[]{:S(2)}, u32[]{:S(2)}) %collective-permute-start.4) | collective-permute-done | bytes 96 | tf_op jit(solution)/shard_map/ppermute | solution.py:45
  103.3 0.7 fusion.33
  (38 shorter events, 2.4 us)
Async XLA Ops:
  0.6 6.3 %copy-start = (bf16[96,64,256]{2,1,0:T(8,128)(2,1)S(1)}, bf16[96,64,256]{2,1,0:T(8,128)(2,1)}, u32[]{:S(2)}) copy-start(bf16[96,64,256]{2,1,0:T(8,128)(2,1)} %param.5) | copy-start | bytes 9437188
  0.6 3.7 %collective-permute-start = (bf16[1,2,64,256]{3,2,1,0:T(8,128)(2,1)}, bf16[1,2,64,256]{3,2,1,0:T(8,128)(2,1)}, u32[]{:S(2)}, u32[]{:S(2)}) collective-permute-start(bf16[1,2,64,256]{3,2,1,0:T(8,128)(2,1)} %bitcast.30), channel_id=1, source_target_pairs={{0,1},{1,0},{2,3},{3,2},{4,5},{5,4},{6,7},{7,6},{8,9},{9,8},{10,11... | collective-permute-start | bytes 196616 | tf_op jit(solution)/shard_map/ppermute | solution.py:29
  5.3 7.8 %collective-permute-start.1 = (bf16[2,2,64,256]{3,2,1,0:T(8,128)(2,1)S(1)}, bf16[2,2,64,256]{3,2,1,0:T(8,128)(2,1)}, u32[]{:S(2)}, u32[]{:S(2)}) collective-permute-start(bf16[2,2,64,256]{3,2,1,0:T(8,128)(2,1)S(1)} %pad_maximum_fusion.3), channel_id=1, source_target_pairs={{0,2},{1,3},{2,0},{3,1},{4,6},{5,7},{6,4},{7,5},{8,10},{9,11},{10,... | collective-permute-start | bytes 393224 | tf_op jit(solution)/shard_map/ppermute | solution.py:29
  14.8 17.9 %collective-permute-start.2 = (bf16[4,2,64,256]{3,2,1,0:T(8,128)(2,1)}, bf16[4,2,64,256]{3,2,1,0:T(8,128)(2,1)}, u32[]{:S(2)}, u32[]{:S(2)}) collective-permute-start(bf16[4,2,64,256]{3,2,1,0:T(8,128)(2,1)} %pad_maximum_fusion.2), channel_id=1, source_target_pairs={{0,4},{1,5},{2,6},{3,7},{4,0},{5,1},{6,2},{7,3},{8,12},{9,13},{10,... | collective-permute-start | bytes 786440 | tf_op jit(solution)/shard_map/ppermute | solution.py:29
  32.7 3.7 %copy-start.8 = (s32[32,1]{0,1:T(1,128)S(1)}, s32[32,1]{0,1:T(1,128)}, u32[]{:S(2)}) copy-start(s32[32,1]{0,1:T(1,128)} %param.9) | copy-start | bytes 388
  33.7 25.2 %collective-permute-start.3 = (bf16[8,2,64,256]{3,2,1,0:T(8,128)(2,1)S(1)}, bf16[8,2,64,256]{3,2,1,0:T(8,128)(2,1)S(1)}, u32[]{:S(2)}, u32[]{:S(2)}) collective-permute-start(bf16[8,2,64,256]{3,2,1,0:T(8,128)(2,1)S(1)} %pad_maximum_fusion.1), channel_id=1, source_target_pairs={{0,8},{1,9},{2,10},{3,11},{4,12},{5,13},{6,14},{7,15},{8,0},{9,1},... | collective-permute-start | bytes 1572872 | tf_op jit(solution)/shard_map/ppermute | solution.py:29
  37.0 22.1 %copy-start.5 = (bf16[256,129]{1,0:T(8,128)(2,1)S(1)}, bf16[256,129]{1,0:T(8,128)(2,1)}, u32[]{:S(2)}) copy-start(bf16[256,129]{1,0:T(8,128)(2,1)} %cosine_convert_fusion) | copy-start | bytes 198148
  37.0 22.1 %copy-start.6 = (bf16[256,127]{1,0:T(8,128)(2,1)S(1)}, bf16[256,127]{1,0:T(8,128)(2,1)}, u32[]{:S(2)}) copy-start(bf16[256,127]{1,0:T(8,128)(2,1)} %fusion.31) | copy-start | bytes 195076
  59.6 1.0 copy-start.2
  69.0 2.7 %copy-start.1 = (bf16[127,96,64]{1,2,0:T(8,128)(2,1)S(1)}, bf16[127,96,64]{1,2,0:T(8,128)(2,1)}, u32[]{:S(2)}) copy-start(bf16[127,96,64]{1,2,0:T(8,128)(2,1)} %copy.31) | copy-start | bytes 4681732
  69.0 2.8 %copy-start.3 = (bf16[127,32,64]{2,1,0:T(8,128)(2,1)S(1)}, bf16[127,32,64]{2,1,0:T(8,128)(2,1)}, u32[]{:S(2)}) copy-start(bf16[127,32,64]{2,1,0:T(8,128)(2,1)} %copy.30) | copy-start | bytes 1560580
  71.7 2.0 %copy-start.4 = (bf16[127,32,64]{2,1,0:T(8,128)(2,1)S(1)}, bf16[127,32,64]{2,1,0:T(8,128)(2,1)}, u32[]{:S(2)}) copy-start(bf16[127,32,64]{2,1,0:T(8,128)(2,1)} %copy.34) | copy-start | bytes 1560580
  93.5 10.5 %copy-start.7 = (f32[32,96]{1,0:T(8,128)}, f32[32,96]{1,0:T(8,128)S(1)}, u32[]{:S(2)}) copy-start(f32[32,96]{1,0:T(8,128)S(1)} %reshape.53) | copy-start | bytes 36868
  93.7 5.7 %collective-permute-start.5 = (f32[1,16]{0,1:T(8,128)S(1)}, f32[1,16]{0,1:T(8,128)S(1)}, u32[]{:S(2)}, u32[]{:S(2)}) collective-permute-start(f32[1,16]{0,1:T(8,128)S(1)} %get-tuple-element.48), channel_id=1, source_target_pairs={{1,0},{2,1},{3,2},{4,3},{5,4},{6,5},{7,6},{8,7},{9,8},{10,9},{11,1... | collective-permute-start | bytes 200 | tf_op jit(solution)/shard_map/ppermute | solution.py:46
  97.5 5.9 %collective-permute-start.4 = (f32[1,16]{0,1:T(8,128)S(1)}, f32[1,16]{0,1:T(8,128)S(1)}, u32[]{:S(2)}, u32[]{:S(2)}) collective-permute-start(f32[1,16]{0,1:T(8,128)S(1)} %get-tuple-element.47), channel_id=1, source_target_pairs={{0,1},{1,2},{2,3},{3,4},{4,5},{5,6},{6,7},{7,8},{8,9},{9,10},{10,1... | collective-permute-start | bytes 200 | tf_op jit(solution)/shard_map/ppermute | solution.py:45
